TPU v7x, 128 devices: a whole 4x4x4 slice. The times are simulated.
128 devices in a mesh: panel: 32 (over z, x, core), obs: 4 (over y).
Axes of the slice: x: 4, y: 4, z: 4, core: 2. Of those that a mesh axis runs over, the one named last changes fastest.
Arguments:
- positions: float32 [3, 1048576], P(None, ('panel', 'obs')), may hold values from -3 to 3
- normals: float32 [3, 1048576], P(None, ('panel', 'obs')), may hold values from -0.6 to 0.6
- mean_flow: float32 [3, 1048576], P(None, ('panel', 'obs')), may hold values from -3 to 3
- harmonics: float32 [2, 10, 1048576], P(None, None, ('panel', 'obs')), may hold values from -6 to 6
- counts: int32 [128], P(('panel', 'obs')), may hold values from 6144 to 8192, as said below
- block_of: int32 [1048576, 1], P(('panel', 'obs')), may hold values from 0 to 31; in each aligned block of 8192 rows (0 to 8191, 8192 to 16383, ...) at most 512 rows name the same one
- observers: float32 [3, 1024], P(None, 'obs'), may hold values from 6 to 24
- wavenumber: float32 [1], replicated, may hold values from 4 to 8
Outputs:
- contributions: float32 [32, 4, 1024], P('panel', None, 'obs')
- total: float32 [4, 1024], P(None, 'obs')
Inputs may be any that keep to these rules, and one draw needn't show every extreme that they name: Each volume partition has 8192 slots, of which the first counts are live; at least one partition has every slot live and one has 6144. `block_of`: among the 8192 slots of one volume partition no panel block is named more than 512 times, and some block is named exactly 512 times.
All inputs are finite; a program needn't handle non-finite values.
Results may differ from a plain program's by a relative error of at most 0.0003.
Values sent between devices are 32-bit elements; how exact they have to be, the bound alone decides.
A program may use at most 64 MiB of HBM per device.

v0:
```python
import math

import jax
import jax.numpy as jnp
from jax import lax
from jax.sharding import PartitionSpec as P

HARMS = 2


def derive(stacked):
    surface = stacked[3:6]
    velocity_mean = stacked[6:9]
    normal_mean = jnp.sum(velocity_mean * surface, axis=0)
    collected = []
    for harmonic in range(HARMS):
        for half in range(2):
            start = 9 + harmonic * 10 + half * 5
            density = stacked[start]
            velocity = stacked[start + 1 : start + 4]
            normal_part = jnp.sum(velocity * surface, axis=0)
            collected.append(normal_part + density * normal_mean)
        for half in range(2):
            start = 9 + harmonic * 10 + half * 5
            velocity = stacked[start + 1 : start + 4]
            pressure = stacked[start + 4]
            normal_part = jnp.sum(velocity * surface, axis=0)
            loading = (
                pressure[None, :] * surface
                + velocity_mean * normal_part[None, :]
                + velocity * normal_mean[None, :]
            )
            collected.extend([loading[0], loading[1], loading[2]])
    return jnp.stack(collected)


def pair_terms(sources, places, watchers, base_number):
    delta_x = watchers[0][:, None] - places[0][None, :]
    delta_y = watchers[1][:, None] - places[1][None, :]
    delta_z = watchers[2][:, None] - places[2][None, :]
    radius = jnp.sqrt(delta_x * delta_x + delta_y * delta_y + delta_z * delta_z)
    inverse = 1.0 / radius
    unit_x = delta_x * inverse
    unit_y = delta_y * inverse
    unit_z = delta_z * inverse
    green_scale = inverse * (0.25 / math.pi)
    collected = []
    for harmonic in range(HARMS):
        number = (harmonic + 1) * base_number
        first = 8 * harmonic
        q_real = sources[first][None, :]
        q_imag = sources[first + 1][None, :]
        along_real = (
            sources[first + 2][None, :] * unit_x
            + sources[first + 3][None, :] * unit_y
            + sources[first + 4][None, :] * unit_z
        )
        along_imag = (
            sources[first + 5][None, :] * unit_x
            + sources[first + 6][None, :] * unit_y
            + sources[first + 7][None, :] * unit_z
        )
        amp_real = -number * (q_imag + along_imag) + along_real * inverse
        amp_imag = number * (q_real + along_real) + along_imag * inverse
        phase = number * radius
        cosine = jnp.cos(phase)
        sine_part = jnp.sin(phase)
        collected.append((amp_real * cosine + amp_imag * sine_part) * green_scale)
        collected.append((amp_imag * cosine - amp_real * sine_part) * green_scale)
    return jnp.stack(collected)


def slot_fold(arrays, fold, initial, watchers_count):
    length = arrays[0].shape[-1]
    width = 8192
    while width > 512 and (length % width != 0 or width * watchers_count > 2097152):
        width = width // 2
    count = length // width

    def step(index, carry):
        piece = tuple(
            (
                lax.dynamic_slice_in_dim(array, index * width, width, array.ndim - 1)
                for array in arrays
            )
        )
        return fold(carry, piece)

    return lax.fori_loop(0, count, step, initial)


def summing(watchers, base_number):

    def fold(carry, piece):
        return carry + jnp.sum(pair_terms(piece[0], piece[1], watchers, base_number), axis=2)

    return fold


def route(stacked, block_of, blocks_total):
    own_slots = stacked.shape[1]
    capacity = 2 * own_slots // blocks_total
    target = block_of[:, 0]
    member = (target[:, None] == jnp.arange(blocks_total, dtype=jnp.int32)[None, :]).astype(
        jnp.int32
    )
    rank = jnp.sum((jnp.cumsum(member, axis=0) - 1) * member, axis=1)
    position = target * capacity + rank
    outgoing = (
        jnp.zeros((stacked.shape[0], blocks_total * capacity), jnp.float32)
        .at[:, position]
        .set(stacked)
    )
    return lax.all_to_all(outgoing, "panel", split_axis=1, concat_axis=1, tiled=True)


def on_device(positions, normals, mean_flow, harmonics, counts, block_of, observers, wavenumber):
    own_slots = positions.shape[1]
    live_mask = (jnp.arange(own_slots, dtype=jnp.int32) < counts[0]).astype(jnp.float32)
    stacked = jnp.concatenate(
        [positions, normals, mean_flow, harmonics.reshape(HARMS * 10, own_slots)], axis=0
    )
    stacked = stacked * live_mask[None, :]
    base_number = wavenumber[0]
    blocks_total = lax.axis_size("panel")
    width = observers.shape[1]
    arrived = route(stacked, block_of, blocks_total)
    sources = derive(arrived)
    packed = jnp.concatenate([arrived[0:3], sources], axis=0)
    folding = summing(observers, base_number)
    initial = jnp.zeros((2 * HARMS, width), jnp.float32)
    piece = lax.all_gather(packed, "obs", axis=1, tiled=True)
    contribution = slot_fold((piece[3:], piece[0:3]), folding, initial, width)[None]
    total = lax.psum(contribution[0], "panel")
    return (contribution, total)


def solution(mesh):
    placed = (
        P(None, ("panel", "obs")),
        P(None, ("panel", "obs")),
        P(None, ("panel", "obs")),
        P(None, None, ("panel", "obs")),
        P(("panel", "obs")),
        P(("panel", "obs"), None),
        P(None, "obs"),
        P(),
    )
    return jax.shard_map(
        on_device,
        mesh=mesh,
        in_specs=placed,
        out_specs=(P("panel", None, "obs"), P(None, "obs")),
        check_vma=False,
    )
```

profile of v0, /device:TPU:0, one launch (start us, length us, event | category | flops | bytes accessed | tf_op | source)
XLA Modules:
  0.0 977.6 jit_solution(4751403590396884583)
XLA Ops:
  7.2 0.0 all-gather.2.cloned.1.call-start
  7.2 1.0 fusion.22
  8.2 9.5 reduce-window.6
  17.8 0.9 slice_reduce_fusion
  18.7 0.2 reduce-window.9
  18.9 0.3 add_add_fusion
  19.2 1.5 fusion.20
  20.7 0.8 compare_select_fusion
  21.5 1.5 copy.26
  23.0 0.1 reshape.1898
  23.8 0.2 fusion.21
  24.1 2.7 copy.27
  26.8 24.5 %scatter_custom_fusion = f32[29,16384]{0,1:T(8,128)} fusion(s32[8192]{0:T(1024)S(1)} %bitcast.203, f32[8192,29]{1,0:T(8,128)} %copy.27, f32[]{:T(128)} %constant.76.clone.1), kind=kCustom, calls=%fused_computation.41 | custom fusion | bytes 1901056 | tf_op jit(solution)/shard_map/scatter | solution.py:112
  51.3 5.2 copy.28
  56.5 36.5 %all_to_all.9 = f32[29,32,512]{2,0,1:T(8,128)S(1)} all-to-all(f32[29,32,512]{2,0,1:T(8,128)S(1)} %copy.28), channel_id=1, replica_groups=mesh['panel'=32,'obs'=4] {'panel'}, dimensions={1} | all-to-all | bytes 3801088 | tf_op jit(solution)/shard_map/all_to_all | solution.py:114
  93.1 1.1 multiply_reduce_fusion
  94.3 0.1 copy.30
  94.3 0.1 copy.31
  94.4 0.1 copy.32
  94.5 0.1 copy.36
  94.6 0.1 copy.37
  94.7 0.4 fusion.26
  95.0 0.3 multiply_add_fusion.9
  95.3 0.5 multiply_add_fusion.5
  95.8 0.0 copy-start.4
  95.8 3.1 concatenate.8
  99.0 0.0 all-gather.2.cloned.1.call-update
  99.6 63.1 %all-gather.2.cloned.1.call-done = f32[19,65536]{1,0:T(8,128)} async-done(((f32[19,16384]{1,0:T(8,128)}), f32[19,65536]{1,0:T(8,128)}) %all-gather.2.cloned.1.call-update) | async-done | bytes 4980752 | tf_op jit(solution)/shard_map/all_gather | solution.py:132
  162.7 5.2 slice.368
  167.9 735.2 %while.15 = (s32[]{:T(128)}, f32[4,256]{1,0:T(4,128)S(1)}, f32[]{:T(128)}, f32[16,65536]{1,0:T(8,128)}, f32[3,256]{1,0:T(4,128)S(1)}, /*index=5*/f32[3,65536]{1,...) while((s32[]{:T(128)}, f32[4,256]{1,0:T(4,128)S(1)}, ...), condition=%wide.region_11.12_spmd.clone, body=%wide.region_9.11_spmd.clone.sunk | while | flops 201327632 | bytes 69104176 | solution.py:89
  167.9 3.8 constant_dynamic-slice_fusion.3
  171.8 43.0 %add_multiply_fusion.5 = (f32[1,256,8192]{2,1,0:T(8,128)S(1)}, f32[1,256,8192]{2,1,0:T(8,128)S(1)}) fusion(f32[]{:T(128)} %get-tuple-element.434, f32[8192]{0:T(1024)S(1)} %bitcast.138, f32[256]{0:T(256)S(1)} %bitcast.196, f32[8192]{0:T(1024)S(1)} %bitcast.136, f32[256]{0:T(256)S(1)} %bitcast.198, f32[8192]{0:T(1024)S(1)} %bitcast.134, ...), kind=kLoop, calls=%fused_computation.29.clone.1 | loop fusion | flops 83886080 | bytes 17140744 | tf_op jit(solution)/shard_map/while/body/eval_jaxpr/mul | solution.py:68
  214.8 42.4 %add_multiply_fusion.4 = (f32[1,256,8192]{2,1,0:T(8,128)S(1)}, f32[1,256,8192]{2,1,0:T(8,128)S(1)}) fusion(f32[]{:T(128)} %get-tuple-element.436, f32[8192]{0:T(1024)S(1)} %bitcast.139, f32[256]{0:T(256)S(1)} %bitcast.197, f32[8192]{0:T(1024)S(1)} %bitcast.137, f32[256]{0:T(256)S(1)} %bitcast.199, f32[8192]{0:T(1024)S(1)} %bitcast.135, ...), kind=kLoop, calls=%fused_computation.12.clone.1 | loop fusion | flops 83886080 | bytes 17140744 | tf_op jit(solution)/shard_map/while/body/eval_jaxpr/mul | solution.py:68
  257.2 2.2 maximum_reduce_fusion.2
  259.5 4.6 constant_dynamic-slice_fusion.3
  264.0 43.0 %add_multiply_fusion.5 = (f32[1,256,8192]{2,1,0:T(8,128)S(1)}, f32[1,256,8192]{2,1,0:T(8,128)S(1)}) fusion(f32[]{:T(128)} %get-tuple-element.434, f32[8192]{0:T(1024)S(1)} %bitcast.138, f32[256]{0:T(256)S(1)} %bitcast.196, f32[8192]{0:T(1024)S(1)} %bitcast.136, f32[256]{0:T(256)S(1)} %bitcast.198, f32[8192]{0:T(1024)S(1)} %bitcast.134, ...), kind=kLoop, calls=%fused_computation.29.clone.1 | loop fusion | flops 83886080 | bytes 17140744 | tf_op jit(solution)/shard_map/while/body/eval_jaxpr/mul | solution.py:68
  307.1 42.4 %add_multiply_fusion.4 = (f32[1,256,8192]{2,1,0:T(8,128)S(1)}, f32[1,256,8192]{2,1,0:T(8,128)S(1)}) fusion(f32[]{:T(128)} %get-tuple-element.436, f32[8192]{0:T(1024)S(1)} %bitcast.139, f32[256]{0:T(256)S(1)} %bitcast.197, f32[8192]{0:T(1024)S(1)} %bitcast.137, f32[256]{0:T(256)S(1)} %bitcast.199, f32[8192]{0:T(1024)S(1)} %bitcast.135, ...), kind=kLoop, calls=%fused_computation.12.clone.1 | loop fusion | flops 83886080 | bytes 17140744 | tf_op jit(solution)/shard_map/while/body/eval_jaxpr/mul | solution.py:68
  349.4 2.2 maximum_reduce_fusion.2
  351.7 4.8 constant_dynamic-slice_fusion.3
  356.5 43.0 %add_multiply_fusion.5 = (f32[1,256,8192]{2,1,0:T(8,128)S(1)}, f32[1,256,8192]{2,1,0:T(8,128)S(1)}) fusion(f32[]{:T(128)} %get-tuple-element.434, f32[8192]{0:T(1024)S(1)} %bitcast.138, f32[256]{0:T(256)S(1)} %bitcast.196, f32[8192]{0:T(1024)S(1)} %bitcast.136, f32[256]{0:T(256)S(1)} %bitcast.198, f32[8192]{0:T(1024)S(1)} %bitcast.134, ...), kind=kLoop, calls=%fused_computation.29.clone.1 | loop fusion | flops 83886080 | bytes 17140744 | tf_op jit(solution)/shard_map/while/body/eval_jaxpr/mul | solution.py:68
  399.5 42.4 %add_multiply_fusion.4 = (f32[1,256,8192]{2,1,0:T(8,128)S(1)}, f32[1,256,8192]{2,1,0:T(8,128)S(1)}) fusion(f32[]{:T(128)} %get-tuple-element.436, f32[8192]{0:T(1024)S(1)} %bitcast.139, f32[256]{0:T(256)S(1)} %bitcast.197, f32[8192]{0:T(1024)S(1)} %bitcast.137, f32[256]{0:T(256)S(1)} %bitcast.199, f32[8192]{0:T(1024)S(1)} %bitcast.135, ...), kind=kLoop, calls=%fused_computation.12.clone.1 | loop fusion | flops 83886080 | bytes 17140744 | tf_op jit(solution)/shard_map/while/body/eval_jaxpr/mul | solution.py:68
  441.9 2.2 maximum_reduce_fusion.2
  444.2 4.2 constant_dynamic-slice_fusion.3
  448.4 43.0 %add_multiply_fusion.5 = (f32[1,256,8192]{2,1,0:T(8,128)S(1)}, f32[1,256,8192]{2,1,0:T(8,128)S(1)}) fusion(f32[]{:T(128)} %get-tuple-element.434, f32[8192]{0:T(1024)S(1)} %bitcast.138, f32[256]{0:T(256)S(1)} %bitcast.196, f32[8192]{0:T(1024)S(1)} %bitcast.136, f32[256]{0:T(256)S(1)} %bitcast.198, f32[8192]{0:T(1024)S(1)} %bitcast.134, ...), kind=kLoop, calls=%fused_computation.29.clone.1 | loop fusion | flops 83886080 | bytes 17140744 | tf_op jit(solution)/shard_map/while/body/eval_jaxpr/mul | solution.py:68
  491.4 42.4 %add_multiply_fusion.4 = (f32[1,256,8192]{2,1,0:T(8,128)S(1)}, f32[1,256,8192]{2,1,0:T(8,128)S(1)}) fusion(f32[]{:T(128)} %get-tuple-element.436, f32[8192]{0:T(1024)S(1)} %bitcast.139, f32[256]{0:T(256)S(1)} %bitcast.197, f32[8192]{0:T(1024)S(1)} %bitcast.137, f32[256]{0:T(256)S(1)} %bitcast.199, f32[8192]{0:T(1024)S(1)} %bitcast.135, ...), kind=kLoop, calls=%fused_computation.12.clone.1 | loop fusion | flops 83886080 | bytes 17140744 | tf_op jit(solution)/shard_map/while/body/eval_jaxpr/mul | solution.py:68
  533.8 2.2 maximum_reduce_fusion.2
  536.1 4.2 constant_dynamic-slice_fusion.3
  540.3 43.0 %add_multiply_fusion.5 = (f32[1,256,8192]{2,1,0:T(8,128)S(1)}, f32[1,256,8192]{2,1,0:T(8,128)S(1)}) fusion(f32[]{:T(128)} %get-tuple-element.434, f32[8192]{0:T(1024)S(1)} %bitcast.138, f32[256]{0:T(256)S(1)} %bitcast.196, f32[8192]{0:T(1024)S(1)} %bitcast.136, f32[256]{0:T(256)S(1)} %bitcast.198, f32[8192]{0:T(1024)S(1)} %bitcast.134, ...), kind=kLoop, calls=%fused_computation.29.clone.1 | loop fusion | flops 83886080 | bytes 17140744 | tf_op jit(solution)/shard_map/while/body/eval_jaxpr/mul | solution.py:68
  583.3 42.4 %add_multiply_fusion.4 = (f32[1,256,8192]{2,1,0:T(8,128)S(1)}, f32[1,256,8192]{2,1,0:T(8,128)S(1)}) fusion(f32[]{:T(128)} %get-tuple-element.436, f32[8192]{0:T(1024)S(1)} %bitcast.139, f32[256]{0:T(256)S(1)} %bitcast.197, f32[8192]{0:T(1024)S(1)} %bitcast.137, f32[256]{0:T(256)S(1)} %bitcast.199, f32[8192]{0:T(1024)S(1)} %bitcast.135, ...), kind=kLoop, calls=%fused_computation.12.clone.1 | loop fusion | flops 83886080 | bytes 17140744 | tf_op jit(solution)/shard_map/while/body/eval_jaxpr/mul | solution.py:68
  625.7 2.2 maximum_reduce_fusion.2
  628.0 3.9 constant_dynamic-slice_fusion.3
  631.8 43.0 %add_multiply_fusion.5 = (f32[1,256,8192]{2,1,0:T(8,128)S(1)}, f32[1,256,8192]{2,1,0:T(8,128)S(1)}) fusion(f32[]{:T(128)} %get-tuple-element.434, f32[8192]{0:T(1024)S(1)} %bitcast.138, f32[256]{0:T(256)S(1)} %bitcast.196, f32[8192]{0:T(1024)S(1)} %bitcast.136, f32[256]{0:T(256)S(1)} %bitcast.198, f32[8192]{0:T(1024)S(1)} %bitcast.134, ...), kind=kLoop, calls=%fused_computation.29.clone.1 | loop fusion | flops 83886080 | bytes 17140744 | tf_op jit(solution)/shard_map/while/body/eval_jaxpr/mul | solution.py:68
  674.9 42.4 %add_multiply_fusion.4 = (f32[1,256,8192]{2,1,0:T(8,128)S(1)}, f32[1,256,8192]{2,1,0:T(8,128)S(1)}) fusion(f32[]{:T(128)} %get-tuple-element.436, f32[8192]{0:T(1024)S(1)} %bitcast.139, f32[256]{0:T(256)S(1)} %bitcast.197, f32[8192]{0:T(1024)S(1)} %bitcast.137, f32[256]{0:T(256)S(1)} %bitcast.199, f32[8192]{0:T(1024)S(1)} %bitcast.135, ...), kind=kLoop, calls=%fused_computation.12.clone.1 | loop fusion | flops 83886080 | bytes 17140744 | tf_op jit(solution)/shard_map/while/body/eval_jaxpr/mul | solution.py:68
  717.3 2.2 maximum_reduce_fusion.2
  719.5 4.0 constant_dynamic-slice_fusion.3
  723.5 43.0 %add_multiply_fusion.5 = (f32[1,256,8192]{2,1,0:T(8,128)S(1)}, f32[1,256,8192]{2,1,0:T(8,128)S(1)}) fusion(f32[]{:T(128)} %get-tuple-element.434, f32[8192]{0:T(1024)S(1)} %bitcast.138, f32[256]{0:T(256)S(1)} %bitcast.196, f32[8192]{0:T(1024)S(1)} %bitcast.136, f32[256]{0:T(256)S(1)} %bitcast.198, f32[8192]{0:T(1024)S(1)} %bitcast.134, ...), kind=kLoop, calls=%fused_computation.29.clone.1 | loop fusion | flops 83886080 | bytes 17140744 | tf_op jit(solution)/shard_map/while/body/eval_jaxpr/mul | solution.py:68
  766.6 42.4 %add_multiply_fusion.4 = (f32[1,256,8192]{2,1,0:T(8,128)S(1)}, f32[1,256,8192]{2,1,0:T(8,128)S(1)}) fusion(f32[]{:T(128)} %get-tuple-element.436, f32[8192]{0:T(1024)S(1)} %bitcast.139, f32[256]{0:T(256)S(1)} %bitcast.197, f32[8192]{0:T(1024)S(1)} %bitcast.137, f32[256]{0:T(256)S(1)} %bitcast.199, f32[8192]{0:T(1024)S(1)} %bitcast.135, ...), kind=kLoop, calls=%fused_computation.12.clone.1 | loop fusion | flops 83886080 | bytes 17140744 | tf_op jit(solution)/shard_map/while/body/eval_jaxpr/mul | solution.py:68
  809.0 2.2 maximum_reduce_fusion.2
  811.2 4.3 constant_dynamic-slice_fusion.3
  815.5 43.0 %add_multiply_fusion.5 = (f32[1,256,8192]{2,1,0:T(8,128)S(1)}, f32[1,256,8192]{2,1,0:T(8,128)S(1)}) fusion(f32[]{:T(128)} %get-tuple-element.434, f32[8192]{0:T(1024)S(1)} %bitcast.138, f32[256]{0:T(256)S(1)} %bitcast.196, f32[8192]{0:T(1024)S(1)} %bitcast.136, f32[256]{0:T(256)S(1)} %bitcast.198, f32[8192]{0:T(1024)S(1)} %bitcast.134, ...), kind=kLoop, calls=%fused_computation.29.clone.1 | loop fusion | flops 83886080 | bytes 17140744 | tf_op jit(solution)/shard_map/while/body/eval_jaxpr/mul | solution.py:68
  858.5 42.4 %add_multiply_fusion.4 = (f32[1,256,8192]{2,1,0:T(8,128)S(1)}, f32[1,256,8192]{2,1,0:T(8,128)S(1)}) fusion(f32[]{:T(128)} %get-tuple-element.436, f32[8192]{0:T(1024)S(1)} %bitcast.139, f32[256]{0:T(256)S(1)} %bitcast.197, f32[8192]{0:T(1024)S(1)} %bitcast.137, f32[256]{0:T(256)S(1)} %bitcast.199, f32[8192]{0:T(1024)S(1)} %bitcast.135, ...), kind=kLoop, calls=%fused_computation.12.clone.1 | loop fusion | flops 83886080 | bytes 17140744 | tf_op jit(solution)/shard_map/while/body/eval_jaxpr/mul | solution.py:68
  900.9 2.2 maximum_reduce_fusion.2
  903.2 0.0 copy-start
  903.2 67.6 %psum.7 = f32[4,256]{1,0:T(4,128)} all-reduce(f32[4,256]{1,0:T(4,128)S(1)} %get-tuple-element.146), channel_id=1, replica_groups=mesh['panel'=32,'obs'=4] {'panel'}, use_global_device_ids=true, to_apply=%region_12.13 | all-reduce | flops 1024 | bytes 8192 | tf_op jit(solution)/shard_map/psum | solution.py:134
  (33 shorter events, 0.3 us)
Async XLA Ops:
  7.2 16.6 %copy-start.3 = (f32[3,8192]{1,0:T(4,128)S(1)}, f32[3,8192]{1,0:T(4,128)}, u32[]{:S(2)}) copy-start(f32[3,8192]{1,0:T(4,128)} %param.10) | copy-start | bytes 294916
  7.2 16.6 %copy-start.2 = (f32[3,8192]{1,0:T(4,128)S(1)}, f32[3,8192]{1,0:T(4,128)}, u32[]{:S(2)}) copy-start(f32[3,8192]{1,0:T(4,128)} %param.11) | copy-start | bytes 294916
  7.2 16.6 %copy-start.1 = (f32[3,8192]{1,0:T(4,128)S(1)}, f32[3,8192]{1,0:T(4,128)}, u32[]{:S(2)}) copy-start(f32[3,8192]{1,0:T(4,128)} %param.12) | copy-start | bytes 294916
  7.2 155.5 %all-gather.2.cloned.1.call-start = ((), (), s32[]{:S(2)}) async-start(), calls=%async_computation.1 | async-start | bytes 7864320 | tf_op jit(solution)/shard_map/all_gather | solution.py:132
  95.8 72.1 %copy-start.4 = (f32[3,256]{1,0:T(4,128)S(1)}, f32[3,256]{1,0:T(4,128)}, u32[]{:S(2)}) copy-start(f32[3,256]{1,0:T(4,128)} %param.16) | copy-start | bytes 9220
  162.7 5.2 slice-start
  903.2 67.6 %copy-start = (f32[4,256]{1,0:T(4,128)}, f32[4,256]{1,0:T(4,128)S(1)}, u32[]{:S(2)}) copy-start(f32[4,256]{1,0:T(4,128)S(1)} %get-tuple-element.146) | copy-start | bytes 12292
Sparse Core Ops, SparseCore 0:
  99.1 63.5 all-gather.1
where the time goes:
time: 978 us
  other arithmetic  716 us (73%)
  blocking collectives  104 us (11%)
  local copies, waits for them, and re-layouts  77.9 us (8%)
  waiting for transfers between devices  63.1 us (6%)
  between operations  15.6 us (2%)
    mul x16, other arithmetic, pair_terms(): collected.append((amp_real * cosine + amp_imag * sine_part) * green_scale)  683 us
    psum x1, blocking collectives, on_device(): total = lax.psum(contribution[0], 'panel')  67.6 us
    all_gather x1, waiting for transfers between devices, on_device(): piece = lax.all_gather(packed, 'obs', axis=1, tiled=True)  63.1 us
    all_to_all x1, blocking collectives, route(): lax.all_to_all(outgoing, 'panel', split_axis=1, concat_axis=1, tiled=True)  36.5 us
    slice x16, local copies, waits for them, and re-layouts, pair_terms(): delta_x = watchers[0][:, None] - places[0][None, :]  33.7 us
    scatter x1, local copies, waits for them, and re-layouts, route(): outgoing = jnp.zeros((stacked.shape[0], blocks_total * capacity), jnp.flo...  24.5 us
  transfers between devices with their start and end apart: 1, of which 1 were waited for; matrix products, arithmetic and copies ran while one was open for 0% of the time, Pallas kernels for 0%

commit v1 on v0

v1 whole, which is shorter than its diff:
```python
import math

import jax
import jax.numpy as jnp
from jax import lax
from jax.experimental import pallas as pl
from jax.experimental.pallas import tpu as pltpu
from jax.sharding import PartitionSpec as P

HARMS = 2
CELLS = 128
STEP = 2 * math.pi / CELLS
GROUP = 16
DEPTH = 32
QUANTITIES = 5
ROWS = QUANTITIES * GROUP
PITCH = 9
BLOCKS = 32
SIDES = 4
EVERYONE = BLOCKS * SIDES
MESH = pl.DeviceIdType.MESH


def pieces(value):
    first = value.astype(jnp.bfloat16).astype(jnp.float32)
    rest = value - first
    second = rest.astype(jnp.bfloat16).astype(jnp.float32)
    third = (rest - second).astype(jnp.bfloat16).astype(jnp.float32)
    return first, second, third


def observer_kernel(wave_ref, own_ref, out_ref, every, send_sem, recv_sem):
    panel, side = lax.axis_index("panel"), lax.axis_index("obs")
    barrier = pltpu.get_barrier_semaphore()
    others = [lax.rem(side + step, SIDES) for step in range(1, SIDES)]
    for other in others:
        pl.semaphore_signal(barrier, inc=1, device_id=(panel, other), device_id_type=MESH)
    pl.semaphore_wait(barrier, SIDES - 1)
    copies = []
    for step, other in enumerate(others):
        copy = pltpu.make_async_remote_copy(
            src_ref=own_ref,
            dst_ref=every.at[side],
            send_sem=send_sem.at[step],
            recv_sem=recv_sem.at[step],
            device_id=(panel, other),
            device_id_type=MESH,
        )
        copy.start()
        copies.append(copy)
    for copy in copies:
        copy.wait()
    every[side] = own_ref[...]
    scale = wave_ref[0] * (1 / STEP)
    width = own_ref.shape[1]
    out_ref[...] = jnp.zeros_like(out_ref)
    for k in range(SIDES):
        scaled = every[k] * scale
        here = pl.ds(k * width, width)
        one = jnp.ones((1, width), jnp.bfloat16)
        rows = []
        for axis in range(3):
            a, b, c = pieces(scaled[axis : axis + 1])
            rows += [a, b, c, a, b, a]
        rows += [one] * 3 + list(pieces(jnp.sum(scaled * scaled, axis=0, keepdims=True)))
        rows = jnp.concatenate(
            [row.astype(jnp.float32) for row in rows]
            + [jnp.zeros((DEPTH - len(rows), width), jnp.float32)],
            axis=0,
        )
        out_ref[:, here] = rows.astype(jnp.bfloat16)


def observer_rows(wavenumber, observers):
    width = observers.shape[1]
    inside = pl.BlockSpec(memory_space=pltpu.VMEM)
    return pl.pallas_call(
        observer_kernel,
        out_shape=jax.ShapeDtypeStruct((DEPTH, SIDES * width), jnp.bfloat16),
        in_specs=[pl.BlockSpec(memory_space=pltpu.SMEM), inside],
        out_specs=inside,
        scratch_shapes=[
            pltpu.VMEM((SIDES, 3, width), jnp.float32),
            pltpu.SemaphoreType.DMA((SIDES - 1,)),
            pltpu.SemaphoreType.DMA((SIDES - 1,)),
        ],
        compiler_params=pltpu.CompilerParams(collective_id=0, has_side_effects=True),
        name="observer_rows",
    )(wavenumber, observers)


def panel_rows(chunk, count_ref, wave_ref, places, normals, flows, amplitudes, feature, rows):
    here = pl.ds(pl.multiple_of(chunk * 128, 128), 128)
    lane = lax.broadcasted_iota(jnp.int32, (1, 128), 1) + chunk * 128
    live = lane < count_ref[0]
    wave = wave_ref[0]

    def masked(value):
        return jnp.where(live, value, 0.0)

    scaled = masked(places[:, here]) * (wave * (1 / STEP))
    surface = masked(normals[:, here])
    flow = masked(flows[:, here])
    normal_mean = jnp.sum(flow * surface, axis=0, keepdims=True)
    base = wave * wave * (0.25 / math.pi)
    which = lax.broadcasted_iota(jnp.int32, (HARMS, 128), 0)
    gain = jnp.where(which == 0, 1.0, 4.0) * base

    def axis_of(value, axis):
        return value[axis : axis + 1]

    def put(quantity, row, values):
        for k, value in enumerate(values):
            feature[quantity, row + k : row + k + 1, :] = value

    for axis in range(3):
        a, b, c = pieces(-2.0 * axis_of(scaled, axis))
        put(0, 6 * axis, (a, a, a, b, b, c))
    put(0, 18, pieces(jnp.sum(scaled * scaled, axis=0, keepdims=True)))
    for half in range(2):
        density, vx, vy, vz, pressure = [masked(amplitudes[half * 5 + v, :, here]) for v in range(5)]
        velocity = (vx, vy, vz)
        normal_part = sum(velocity[axis] * axis_of(surface, axis) for axis in range(3))
        strength = (normal_part + density * normal_mean) * gain
        constant = jnp.zeros_like(strength)
        values = []
        for axis in range(3):
            loading = (
                pressure * axis_of(surface, axis)
                + axis_of(flow, axis) * normal_part
                + velocity[axis] * normal_mean
            ) * gain
            constant = constant - loading * axis_of(scaled, axis)
            a, b, c = pieces(loading)
            values.append((6 * axis, (a, a, a, b, b, c)))
        values.append((18, pieces(constant)))
        values.append((24, pieces(strength)))
        for row, columns in values:
            for h in range(HARMS):
                put(1 + 2 * h + half, row, [axis_of(column, h) for column in columns])
    for quantity in range(QUANTITIES):
        turned = feature[quantity].T.astype(jnp.bfloat16)
        for group in range(128 // GROUP):
            rows[chunk * (128 // GROUP) + group, pl.ds(quantity * GROUP, GROUP), :] = turned[
                group * GROUP : (group + 1) * GROUP
            ]


def lookup(table, index):
    numbers = lax.GatherDimensionNumbers(
        offset_dims=(),
        collapsed_slice_dims=(1,),
        start_index_map=(1,),
        operand_batching_dims=(0,),
        start_indices_batching_dims=(0,),
    )
    return lax.gather(
        table, index[..., None], numbers, (1, 1), mode=lax.GatherScatterMode.PROMISE_IN_BOUNDS
    )


def pair_kernel(
    count_ref,
    wave_ref,
    block_ref,
    places,
    normals,
    flows,
    amplitudes,
    observer_ref,
    ones_ref,
    table_ref,
    out_ref,
    feature,
    rows,
    sums,
    big,
    small,
):
    groups = rows.shape[0]
    sums[...] = jnp.zeros_like(sums)
    feature[...] = jnp.zeros_like(feature)
    feature[0, 21:24, :] = jnp.ones((3, 128), jnp.float32)

    def prepare(chunk, _):
        panel_rows(chunk, count_ref, wave_ref, places, normals, flows, amplitudes, feature, rows)
        return 0

    lax.fori_loop(0, groups * GROUP // 128, prepare, 0)

    def produce(group, slot):
        values = jnp.dot(rows[group], observer_ref[...], preferred_element_type=jnp.float32)
        for row in range(ROWS // 8):
            for tile in range(8):
                big[slot, pl.ds(row * 8 * PITCH + tile * PITCH, 8), :] = values[
                    8 * row : 8 * row + 8, 128 * tile : 128 * tile + 128
                ]
        small[slot] = jnp.dot(
            rows[group, GROUP:, :], ones_ref[...], preferred_element_type=jnp.float32
        )

    def consume(group, slot):
        for i in range(GROUP):

            def quantity(q):
                row = q * GROUP + i
                return big[slot, pl.ds((row // 8) * 8 * PITCH + row % 8, 8, stride=PITCH), :]

            def strength(q):
                return jnp.broadcast_to(small[slot, pl.ds(q * GROUP + i, 1), :], (8, 128))

            square = quantity(0)
            inverse = lax.rsqrt(square)
            cells = square * inverse
            nearest = jnp.round(cells).astype(jnp.int32)
            rest = cells - nearest.astype(jnp.float32)
            index = nearest & (CELLS - 1)
            cos_cell = lookup(table_ref[0], index)
            sin_cell = lookup(table_ref[1], index)
            rest2 = rest * rest
            cos_rest = 1.0 - (STEP * STEP / 2) * rest2
            sin_rest = rest * (STEP - (STEP**3 / 6) * rest2)
            cosine = cos_cell * cos_rest - sin_cell * sin_rest
            sine = sin_cell * cos_rest + cos_cell * sin_rest
            near = inverse * (1 / STEP)
            half = inverse * (0.5 / STEP)
            near_cos = near * cosine
            near_sin = near * sine
            double_cos = half - sine * near_sin
            double_sin = sine * near_cos
            place = pl.multiple_of(block_ref[group * GROUP + i] * 32, 8)
            for harmonic, (cosw, sinw, weight) in enumerate(
                ((near_cos, near_sin, near), (double_cos, double_sin, half))
            ):
                q = 2 * harmonic
                along_real = quantity(1 + q) * inverse
                along_imag = quantity(2 + q) * inverse
                amp_real = along_real * weight - (strength(q + 1) + along_imag)
                amp_imag = along_imag * weight + (strength(q) + along_real)
                sums[pl.ds(place + 8 * q, 8), :] += amp_real * cosw + amp_imag * sinw
                sums[pl.ds(place + 8 * q + 8, 8), :] += amp_imag * cosw - amp_real * sinw

    produce(0, 0)

    def body(i, _):
        produce(2 * i + 1, 1)
        consume(2 * i, 0)
        produce(jnp.minimum(2 * i + 2, groups - 1), 0)
        consume(2 * i + 1, 1)
        return 0

    lax.fori_loop(0, groups // 2, body, 0)

    def arrange(block, _):
        for q in range(2 * HARMS):
            value = sums[pl.ds(pl.multiple_of(block * 32 + q * 8, 8), 8), :]
            for side in range(SIDES):
                out_ref[block * SIDES + side, 2 * q : 2 * q + 2, :] = value[2 * side : 2 * side + 2]
        return 0

    lax.fori_loop(0, BLOCKS, arrange, 0)


def pairs(count, wavenumber, block, positions, normals, mean_flow, harmonics, observer_table):
    slots = positions.shape[1]
    ones = jnp.zeros((DEPTH, 128), jnp.bfloat16).at[24:27].set(1.0)
    angle = STEP * jnp.arange(CELLS, dtype=jnp.float32)
    table = jnp.broadcast_to(
        jnp.stack([jnp.cos(angle), jnp.sin(angle)])[:, None, :], (2, 8, CELLS)
    )
    inside = pl.BlockSpec(memory_space=pltpu.VMEM)
    return pl.pallas_call(
        pair_kernel,
        out_shape=jax.ShapeDtypeStruct((EVERYONE, 8, 128), jnp.float32),
        in_specs=[pl.BlockSpec(memory_space=pltpu.SMEM)] * 3 + [inside] * 7,
        out_specs=inside,
        scratch_shapes=[
            pltpu.VMEM((QUANTITIES, DEPTH, 128), jnp.float32),
            pltpu.VMEM((slots // GROUP, ROWS, DEPTH), jnp.bfloat16),
            pltpu.VMEM((BLOCKS * 2 * HARMS * 8, 128), jnp.float32),
            pltpu.VMEM((2, ROWS * PITCH, 128), jnp.float32),
            pltpu.VMEM((2, ROWS - GROUP, 128), jnp.float32),
        ],
        compiler_params=pltpu.CompilerParams(vmem_limit_bytes=48 * 2**20),
        name="pairs",
    )(count, wavenumber, block, positions, normals, mean_flow, harmonics, observer_table, ones, table)


def share_kernel(tiles, out_ref, total_ref, arrived, mine, shared, sems):
    panel, side = lax.axis_index("panel"), lax.axis_index("obs")
    me = panel * SIDES + side
    barrier = pltpu.get_barrier_semaphore()

    def place(step):
        return lax.rem(me + step, EVERYONE)

    def greet(step, _):
        other = place(step)
        pl.semaphore_signal(
            barrier, inc=1, device_id=(other // SIDES, other % SIDES), device_id_type=MESH
        )
        return 0

    lax.fori_loop(1, EVERYONE, greet, 0)
    pl.semaphore_wait(barrier, EVERYONE - 1)

    def send(step, _):
        other = place(step)
        pltpu.make_async_remote_copy(
            src_ref=tiles.at[other],
            dst_ref=arrived.at[step - 1],
            send_sem=sems.at[0],
            recv_sem=sems.at[1],
            device_id=(other // SIDES, other % SIDES),
            device_id_type=MESH,
        ).start()
        return 0

    lax.fori_loop(1, EVERYONE, send, 0)
    everything = pltpu.make_async_remote_copy(
        src_ref=arrived,
        dst_ref=arrived,
        send_sem=sems.at[0],
        recv_sem=sems.at[1],
        device_id=(panel, side),
        device_id_type=MESH,
    )
    everything.wait_recv()
    value = jnp.sum(arrived[...], axis=0) + tiles[me]
    mine[...] = value

    def pass_on(step, _):
        other = lax.rem(panel + step, BLOCKS)
        pltpu.make_async_remote_copy(
            src_ref=mine,
            dst_ref=shared.at[step - 1],
            send_sem=sems.at[2],
            recv_sem=sems.at[3],
            device_id=(other, side),
            device_id_type=MESH,
        ).start()
        return 0

    lax.fori_loop(1, BLOCKS, pass_on, 0)
    for q in range(2 * HARMS):
        for part in range(2):
            row = 2 * q + part
            out_ref[0, q : q + 1, 128 * part : 128 * part + 128] = value[row : row + 1]
    again = pltpu.make_async_remote_copy(
        src_ref=shared,
        dst_ref=shared,
        send_sem=sems.at[2],
        recv_sem=sems.at[3],
        device_id=(panel, side),
        device_id_type=MESH,
    )
    again.wait_recv()

    def add(block, total):
        step = lax.rem(panel - block + BLOCKS, BLOCKS)
        other = shared[jnp.maximum(step - 1, 0)]
        return total + jnp.where(step == 0, value, other)

    total = lax.fori_loop(0, BLOCKS, add, jnp.zeros_like(value))
    for q in range(2 * HARMS):
        for part in range(2):
            row = 2 * q + part
            total_ref[q : q + 1, 128 * part : 128 * part + 128] = total[row : row + 1]
    everything.wait_send()
    again.wait_send()


def share(tiles):
    inside = pl.BlockSpec(memory_space=pltpu.VMEM)
    return pl.pallas_call(
        share_kernel,
        out_shape=(
            jax.ShapeDtypeStruct((1, 2 * HARMS, 256), jnp.float32),
            jax.ShapeDtypeStruct((2 * HARMS, 256), jnp.float32),
        ),
        in_specs=[inside],
        out_specs=(inside, inside),
        scratch_shapes=[
            pltpu.VMEM((EVERYONE - 1, 8, 128), jnp.float32),
            pltpu.VMEM((8, 128), jnp.float32),
            pltpu.VMEM((BLOCKS - 1, 8, 128), jnp.float32),
            pltpu.SemaphoreType.DMA((4,)),
        ],
        compiler_params=pltpu.CompilerParams(collective_id=1, has_side_effects=True),
        name="share",
    )(tiles)


def on_device(positions, normals, mean_flow, harmonics, counts, block_of, observers, wavenumber):
    observer_table = observer_rows(wavenumber, observers)
    amplitudes = harmonics.transpose(1, 0, 2)
    tiles = pairs(
        counts,
        wavenumber,
        block_of[:, 0],
        positions,
        normals,
        mean_flow,
        amplitudes,
        observer_table,
    )
    return share(tiles)


def solution(mesh):
    placed = (
        P(None, ("panel", "obs")),
        P(None, ("panel", "obs")),
        P(None, ("panel", "obs")),
        P(None, None, ("panel", "obs")),
        P(("panel", "obs")),
        P(("panel", "obs"), None),
        P(None, "obs"),
        P(),
    )
    return jax.shard_map(
        on_device,
        mesh=mesh,
        in_specs=placed,
        out_specs=(P("panel", None, "obs"), P(None, "obs")),
        check_vma=False,
    )
```

time: 978 us -> 151 us (0.15)
  other arithmetic: 716 us -> 0.06 us
  Pallas kernels: 0 us -> 140 us
  blocking collectives: 104 us -> 0 us
  local copies, waits for them, and re-layouts: 77.9 us -> 7.31 us
  waiting for transfers between devices: 63.1 us -> 0 us
  between operations: 15.6 us -> 2.02 us
    mul x17 -> x0, other arithmetic: 683 us -> none  [the longest x16 683 us: pair_terms(): collected.append((amp_real * cosine + amp_imag * sine_part) * green_scale)]
    pallas_call x0 -> x3, Pallas kernels: none -> 140 us  [the longest x1 107 us: pairs(): pl.pallas_call(pair_kernel, out_shape=jax.ShapeDtypeStruct((EVERYONE, 8,...]
    psum x1 -> x0, blocking collectives: 67.6 us -> none  [on_device(): total = lax.psum(contribution[0], 'panel')]
    all_gather x1 -> x0, waiting for transfers between devices: 63.1 us -> none  [on_device(): piece = lax.all_gather(packed, 'obs', axis=1, tiled=True)]
    slice x20 -> x0, local copies, waits for them, and re-layouts: 39.4 us -> none  [the longest x16 33.7 us: pair_terms(): delta_x = watchers[0][:, None] - places[0][None, :]]
    all_to_all x1 -> x0, blocking collectives: 36.5 us -> none  [route(): lax.all_to_all(outgoing, 'panel', split_axis=1, concat_axis=1, tiled=True)]
    scatter x1 -> x0, local copies, waits for them, and re-layouts: 24.5 us -> none  [route(): outgoing = jnp.zeros((stacked.shape[0], blocks_total * capacity), jnp.flo...]
    reduce_sum x10 -> x0, other arithmetic: 20.2 us -> none  [the longest x8 17.7 us: fold(): jnp.sum(pair_terms(piece[0], piece[1], watchers, base_number), axis=2)]
  transfers between devices with their start and end apart: 1 -> 0, of which waited for: 1 -> 0; matrix products, arithmetic and copies ran while one was open for 0% -> 0% of each run, Pallas kernels for 0% -> 0%
where the time goes in v1:
time: 151 us; the launch traced here: 150 us
  Pallas kernels  140 us (93%)
  local copies, waits for them, and re-layouts  7.31 us (5%)
  between operations  2.02 us (1%)
    pallas_call x1, Pallas kernels, pairs(): pl.pallas_call(pair_kernel, out_shape=jax.ShapeDtypeStruct((EVERYONE, 8,...  107 us
    pallas_call x1, Pallas kernels, share(): pl.pallas_call(share_kernel, out_shape=(jax.ShapeDtypeStruct((1, 2 * HARM...  25.8 us
    pallas_call x1, Pallas kernels, observer_rows(): pl.pallas_call(observer_kernel, out_shape=jax.ShapeDtypeStruct((DEPTH, SI...  7.75 us
    unnamed x20, local copies, waits for them, and re-layouts  7.31 us

profile of v1, /device:TPU:0, one launch (start us, length us, event | category | flops | bytes accessed | tf_op | source)
XLA Modules:
  0.0 149.7 jit_solution(11330054465905208476)
XLA Ops:
  2.0 0.0 copy-start.6
  2.0 0.0 copy-start.7
  2.0 7.7 %observer_rows.1.observer_ref = bf16[32,1024]{1,0:T(8,128)(2,1)} custom-call(f32[1]{0:T(128)S(6)} %copy.13.wave_ref, f32[3,256]{1,0:T(4,128)} %own_ref.1), custom_call_target="tpu_custom_call" | custom-call | tf_op jit(solution)/shard_map/observer_rows/pallas_call | solution.py:77
  9.8 0.0 copy-done.6
  9.8 0.0 copy-done.7
  9.8 0.0 copy-start.1
  9.8 1.1 copy-done.1
  10.9 0.0 copy-start.2
  10.9 0.8 copy-done.2
  11.7 0.0 copy-start.3
  11.7 0.9 copy-done.3
  12.6 0.0 copy-start.4
  12.6 0.9 copy-done.4
  13.5 0.0 copy-start.5
  13.5 0.9 copy-done.5
  14.4 106.7 %pairs.1.tiles = f32[128,8,128]{2,1,0:T(8,128)S(1)} custom-call(s32[1]{0:T(128)S(6)} %copy.12.count_ref, f32[1]{0:T(128)S(6)} %copy.13.wave_ref, s32[8192]{0:T(1024)S(1)} %bitcast.3, f32[3,8192]{1,0:T(4,128)S(1)} %copy-done.3, f32[3,8192]{1,0:T(4,128)S(1)} %copy-done.4, f32[3,8192]{1,0:T(4,128)S(1)} %copy-done.5, f32[10,2,8192]{2,1,0:T(2,128)S(1)} %bitcast.2, ...), custom_call_target="tpu_custom_call" | custom-call | tf_op jit(solution)/shard_map/pairs/pallas_call | solution.py:272
  121.2 0.0 copy-start
  121.2 0.8 copy-done
  122.0 25.8 %share.1 = (f32[1,4,256]{2,1,0:T(4,128)}, f32[4,256]{1,0:T(4,128)}) custom-call(f32[128,8,128]{2,1,0:T(8,128)} %copy-done), custom_call_target="tpu_custom_call" | custom-call | tf_op jit(solution)/shard_map/share/pallas_call | solution.py:375
  147.8 0.0 copy-start.8
  147.8 1.3 copy.14
  149.1 0.0 copy-done.8
  149.1 0.6 copy.15
  (3 shorter events, 0.1 us)
Async XLA Ops:
  2.0 7.8 %copy-start.6 = (s32[8192,1]{0,1:T(1,128)S(1)}, s32[8192,1]{0,1:T(1,128)}, u32[]{:S(2)}) copy-start(s32[8192,1]{0,1:T(1,128)} %param.15) | copy-start | bytes 98308
  2.0 7.8 %copy-start.7 = (bf16[32,128]{1,0:T(8,128)(2,1)S(1)}, bf16[32,128]{1,0:T(8,128)(2,1)}, u32[]{:S(2)}) copy-start(bf16[32,128]{1,0:T(8,128)(2,1)} %constant.31.clone.1.ones_ref) | copy-start | bytes 24580
  9.8 1.1 copy-start.1
  10.9 0.8 copy-start.2
  11.7 0.9 copy-start.3
  12.6 0.9 copy-start.4
  13.5 0.9 copy-start.5
  121.2 0.8 copy-start
  147.8 1.3 copy-start.8
